TPU v7x, 128 devices: a whole 4x4x4 slice. The times are simulated.
128 devices in a mesh: row: 16 (over y, x_hi, core), col: 8 (over z, x_lo).
Axes of the slice: x: 4 (x_hi: 2, x_lo: 2; x = x_hi * 2 + x_lo), y: 4, z: 4, core: 2. Of those that a mesh axis runs over, the one named last changes fastest.
Arguments:
- layer_input: bfloat16 [8192, 8192], P('row', 'col'), may hold values from -48 to 48
- w_query: bfloat16 [8192, 8192], P('row', 'col'), may hold values from -0.0625 to 0.0625
- w_key: bfloat16 [8192, 1024], P('row', 'col'), may hold values from -0.0625 to 0.0625
- w_value: bfloat16 [8192, 1024], P('row', 'col'), may hold values from -0.0625 to 0.0625
- counts: int32 [64], replicated, may hold values from 1 to 128
- pattern: int32 [64, 4], P('row'), may hold values from 0 to 63, as said below
- cotangent: bfloat16 [8192, 8192], P('row', 'col'), may hold values from -6 to 6
Outputs:
- attended: bfloat16 [8192, 8192], P('row', 'col')
- input_grad: bfloat16 [8192, 8192], P('row', 'col')
Inputs may be any that keep to these rules, and one draw needn't show every extreme that they name: `pattern`: row b lists 4 different blocks, b itself first; every entry lies at a cyclic distance of at most 4 blocks from b, and the second entry exactly at that distance.
All inputs are finite; a program needn't handle non-finite values.
Results may differ from a plain program's by a relative error of at most 0.035.
The roundings to bfloat16 on the way count: a program that leaves them out, or rounds other values in their place, can miss the bound.
Values may be sent and summed in bfloat16 or wider, within the bound.
A program may use at most 128 MiB of HBM per device.

v0:
```python
import jax
import jax.numpy as jnp
from jax import lax
from jax.sharding import PartitionSpec as P

HEADS = 64
KV_HEADS = 8
HEAD_DIM = 128
BLOCK = 128


def padded(block, sides, width):
    for axis, dim in sides:
        count = lax.axis_size(axis)
        forward = [(i, i + 1) for i in range(count - 1)]
        forward.append((count - 1, 0))
        backward = [(target, source) for source, target in forward]
        low = lax.ppermute(
            lax.slice_in_dim(block, block.shape[dim] - width, None, axis=dim), axis, forward
        )
        high = lax.ppermute(lax.slice_in_dim(block, 0, width, axis=dim), axis, backward)
        block = jnp.concatenate([low, block, high], axis=dim)
    return block


def shifted(block, axis, distance):
    devices = range(lax.axis_size(axis))
    route = [((i - distance) % len(devices), i) for i in devices]
    return lax.ppermute(block, axis, route)


def body(layer_input, w_query, w_key, w_value, counts, pattern, cotangent):
    score_scale = HEAD_DIM ** (-0.5)
    group_size = HEADS // KV_HEADS
    tok_rows = layer_input.shape[0]
    per_dev = tok_rows // BLOCK
    block_count = per_dev * lax.axis_size("row")
    myself = lax.axis_index("row")
    all_features = lax.all_gather(layer_input, "col", axis=1, tiled=True)
    full_query = lax.all_gather(w_query, "row", axis=0, tiled=True)
    full_key = lax.all_gather(w_key, "row", axis=0, tiled=True)
    full_value = lax.all_gather(w_value, "row", axis=0, tiled=True)
    query = jnp.dot(all_features, full_query, preferred_element_type=jnp.float32).astype(
        jnp.bfloat16
    )
    keys = jnp.dot(all_features, full_key, preferred_element_type=jnp.float32).astype(jnp.bfloat16)
    values = jnp.dot(all_features, full_value, preferred_element_type=jnp.float32).astype(
        jnp.bfloat16
    )
    kv_heads = keys.shape[1] // HEAD_DIM
    kv_cols = kv_heads * HEAD_DIM
    joined = jnp.concatenate([keys, values], axis=1)
    source = padded(joined, (("row", 0),), tok_rows)
    first_block = myself * per_dev - per_dev
    span_blocks = 3 * per_dev
    nearby = pattern.shape[1]
    local_index = jnp.mod(pattern - first_block, block_count)
    stacked = source.reshape(span_blocks, BLOCK, 2 * kv_cols)
    picked = jnp.take(stacked, local_index, axis=0).reshape(
        per_dev, nearby * BLOCK, 2, kv_heads, HEAD_DIM
    )
    key_blocks = picked[:, :, 0]
    value_blocks = picked[:, :, 1]
    positions = jnp.arange(BLOCK, dtype=jnp.int32)
    key_counts = jnp.take(counts, pattern, axis=0)
    key_live = (positions[None, None, :] < key_counts[:, :, None]).reshape(per_dev, nearby * BLOCK)
    own_counts = lax.dynamic_slice_in_dim(counts, myself * per_dev, per_dev)
    query_live = (positions[None, :] < own_counts[:, None])[:, :, None, None, None]
    query_blocks = query.reshape(per_dev, BLOCK, kv_heads, group_size, HEAD_DIM)
    scores = (
        jnp.einsum(
            "bqkgd,bjkd->bkgqj", query_blocks, key_blocks, preferred_element_type=jnp.float32
        )
        * score_scale
    )
    scores = jnp.where(key_live[:, None, None, None, :], scores, -1e30)
    score_max = jnp.max(scores, axis=-1, keepdims=True)
    exponent = jnp.exp(scores - score_max)
    prob_full = exponent / jnp.sum(exponent, axis=-1, keepdims=True)
    probs_low = prob_full.astype(jnp.bfloat16)
    mixed_out = jnp.einsum(
        "bkgqj,bjkd->bqkgd", probs_low, value_blocks, preferred_element_type=jnp.float32
    )
    attended = (mixed_out * query_live.astype(jnp.float32)).astype(jnp.bfloat16)
    grad_out = cotangent.reshape(
        per_dev, BLOCK, kv_heads, group_size, HEAD_DIM
    ) * query_live.astype(jnp.bfloat16)
    row_delta = jnp.einsum(
        "bqkgd,bqkgd->bkgq", grad_out, attended, preferred_element_type=jnp.float32
    )
    grad_probs = jnp.einsum(
        "bqkgd,bjkd->bkgqj", grad_out, value_blocks, preferred_element_type=jnp.float32
    )
    grad_scores = (prob_full * (grad_probs - row_delta[..., None]) * score_scale).astype(
        jnp.bfloat16
    )
    grad_query = jnp.einsum(
        "bkgqj,bjkd->bqkgd", grad_scores, key_blocks, preferred_element_type=jnp.float32
    )
    grad_query = grad_query.astype(jnp.bfloat16).reshape(tok_rows, -1)
    key_part = jnp.einsum(
        "bkgqj,bqkgd->bjkd", grad_scores, query_blocks, preferred_element_type=jnp.float32
    )
    value_part = jnp.einsum(
        "bkgqj,bqkgd->bjkd", probs_low, grad_out, preferred_element_type=jnp.float32
    )
    grad_parts = jnp.concatenate(
        [
            key_part.reshape(per_dev * nearby, BLOCK, kv_cols),
            value_part.reshape(per_dev * nearby, BLOCK, kv_cols),
        ],
        axis=-1,
    )
    owed_grads = (
        jnp.zeros((span_blocks, BLOCK, 2 * kv_cols), jnp.float32)
        .at[local_index.reshape(-1)]
        .add(grad_parts)
    )
    from_next = shifted(owed_grads[:per_dev].astype(jnp.bfloat16), "row", -1).astype(jnp.float32)
    from_prev = shifted(owed_grads[2 * per_dev :].astype(jnp.bfloat16), "row", 1).astype(
        jnp.float32
    )
    settled = owed_grads[per_dev : 2 * per_dev] + from_next + from_prev
    settled = settled.reshape(tok_rows, 2 * kv_cols)
    grad_keys = settled[:, :kv_cols].astype(jnp.bfloat16)
    grad_values = settled[:, kv_cols:].astype(jnp.bfloat16)
    contract = (((1,), (1,)), ((), ()))
    partial_grad = lax.dot_general(
        grad_query, full_query, contract, preferred_element_type=jnp.float32
    )
    partial_grad = partial_grad + lax.dot_general(
        grad_keys, full_key, contract, preferred_element_type=jnp.float32
    )
    partial_grad = partial_grad + lax.dot_general(
        grad_values, full_value, contract, preferred_element_type=jnp.float32
    )
    input_grad = lax.psum_scatter(
        partial_grad.astype(jnp.bfloat16), "col", scatter_dimension=1, tiled=True
    )
    return (attended.reshape(tok_rows, -1), input_grad)


def solution(mesh):
    placed = (
        P("row", "col"),
        P("row", "col"),
        P("row", "col"),
        P("row", "col"),
        P(),
        P("row", None),
        P("row", "col"),
    )
    return jax.shard_map(
        body,
        mesh=mesh,
        in_specs=placed,
        out_specs=(P("row", "col"), P("row", "col")),
        check_vma=False,
    )
```

profile of v0, /device:TPU:1, one launch (start us, length us, event | category | flops | bytes accessed | tf_op | source)
XLA Modules:
  0.0 668.0 jit_solution(15478223276111546973)
XLA Ops:
  7.2 0.7 all-gather.9.cloned.1.call-update
  7.9 0.7 all-gather.5.cloned.1.call-update
  8.6 0.0 all-gather.7.cloned.1.call-start
  8.7 0.7 all-gather.7.cloned.1.call-update
  9.4 0.5 all-gather.11.cloned.1.call-update
  10.0 0.0 reduce-scatter.2.cloned.1.call-start
  10.0 0.7 compare_select_fusion
  10.7 0.1 reshape.230
  10.8 0.7 compare_and_fusion
  11.5 0.1 reshape.215
  11.6 0.1 reshape.222
  11.7 0.7 dynamic_slice.3
  12.4 1.3 gather_fusion.1
  13.7 0.1 reshape.229
  13.8 0.1 broadcast_bitcast_fusion.1
  13.9 0.1 fusion.36
  14.0 0.7 and_select_fusion
  14.6 0.1 broadcast_bitcast_fusion
  14.7 46.9 %all-gather.9.cloned.1.call-done = bf16[8192,128]{1,0:T(8,128)(2,1)} async-done(((bf16[512,128]{1,0:T(8,128)(2,1)}), bf16[8192,128]{1,0:T(8,128)(2,1)}) %all-gather.9.cloned.1.call-update) | async-done | bytes 2097168 | tf_op jit(solution)/shard_map/all_gather | solution.py:42
  61.6 168.4 %all-gather.5.cloned.1.call-done = bf16[512,8192]{1,0:T(8,128)(2,1)} async-done(((bf16[512,1024]{1,0:T(8,128)(2,1)}), bf16[512,8192]{1,0:T(8,128)(2,1)}) %all-gather.5.cloned.1.call-update) | async-done | bytes 8388624 | tf_op jit(solution)/shard_map/all_gather | solution.py:39
  230.0 6.9 %convolution_convert_fusion.2 = bf16[512,128]{0,1:T(8,128)(2,1)S(1)} fusion(bf16[512,8192]{1,0:T(8,128)(2,1)} %all-gather.5.cloned.1.call-done, bf16[8192,128]{1,0:T(8,128)(2,1)} %all-gather.9.cloned.1.call-done), kind=kOutput, calls=%fused_computation.31 | convolution fusion | flops 1073807360 | bytes 10616832 | tf_op jit(solution)/shard_map/dot_general | solution.py:47
  236.8 44.6 %all-gather.7.cloned.1.call-done = bf16[8192,128]{1,0:T(8,128)(2,1)} async-done(((bf16[512,128]{1,0:T(8,128)(2,1)}), bf16[8192,128]{1,0:T(8,128)(2,1)}) %all-gather.7.cloned.1.call-update) | async-done | bytes 2097168 | tf_op jit(solution)/shard_map/all_gather | solution.py:41
  281.4 6.9 %convolution_convert_fusion.3 = bf16[512,128]{0,1:T(8,128)(2,1)S(1)} fusion(bf16[512,8192]{1,0:T(8,128)(2,1)} %all-gather.5.cloned.1.call-done, bf16[8192,128]{1,0:T(8,128)(2,1)} %all-gather.7.cloned.1.call-done), kind=kOutput, calls=%fused_computation.32 | convolution fusion | flops 1073807360 | bytes 10616832 | tf_op jit(solution)/shard_map/dot_general | solution.py:46
  288.3 0.3 collective-permute-start.1
  288.6 3.0 collective-permute-start
  291.6 0.3 copy.63
  291.9 1.6 copy.25
  293.5 5.3 collective-permute-done.1
  298.8 2.7 collective-permute-done
  301.5 0.1 pad_maximum_fusion.1
  301.6 0.3 copy.19
  301.8 0.6 gather_fusion
  302.4 0.3 gather.11
  302.7 0.5 copy_select_fusion
  303.2 91.0 %all-gather.11.cloned.1.call-done = bf16[8192,1024]{1,0:T(8,128)(2,1)} async-done(((bf16[512,1024]{1,0:T(8,128)(2,1)}), bf16[8192,1024]{1,0:T(8,128)(2,1)}) %all-gather.11.cloned.1.call-update) | async-done | bytes 16777232 | tf_op jit(solution)/shard_map/all_gather | solution.py:40
  394.3 14.8 %fusion.16 = bf16[64,8,8,128]{3,1,2,0:T(8,128)(2,1)S(1)} fusion(bf16[512,8192]{1,0:T(8,128)(2,1)} %all-gather.5.cloned.1.call-done, bf16[8192,1024]{1,0:T(8,128)(2,1)} %all-gather.11.cloned.1.call-done), kind=kOutput, calls=%fused_computation.27 | convolution fusion | flops 8590458880 | bytes 26214400 | tf_op jit(solution)/shard_map/dot_general | solution.py:43
  409.0 0.3 copy.61
  409.3 1.9 bitcast_reduce_fusion
  411.2 1.9 fusion.5
  413.2 4.3 fusion.18
  417.5 4.0 fusion.12
  421.4 3.7 fusion.6
  425.2 2.0 copy-done
  427.1 1.8 fusion.17
  428.9 8.0 %copy.49 = bf16[4,8,128,512]{3,1,2,0:T(8,128)(2,1)} copy(bf16[4,8,128,512]{2,3,1,0:T(8,128)(2,1)} %copy-done) | data formatting | bytes 8388608 | tf_op jit(solution)/shard_map/reshape.34
  436.9 0.3 copy.34
  437.2 3.1 convolution_bitcast_fusion
  440.3 0.3 copy.32
  440.6 2.4 copy.29
  443.0 1.5 pad_maximum_fusion
  444.5 0.1 broadcast_in_dim.52
  444.7 3.5 scatter_fusion
  448.2 0.1 convert.8
  448.3 0.7 fusion.42
  449.0 0.2 collective-permute-start.2
  449.3 3.0 collective-permute-start.3
  452.3 15.7 %fusion.21 = f32[512,8192]{1,0:T(8,128)} fusion(bf16[8192,1024]{1,0:T(8,128)(2,1)} %all-gather.11.cloned.1.call-done, bf16[64,8,8,128]{3,2,1,0:T(8,128)(2,1)S(1)} %bitcast.184), kind=kOutput, calls=%fused_computation.33 | convolution fusion | flops 8589934592 | bytes 34603008 | tf_op jit(solution)/shard_map/dot_general | solution.py:128
  468.0 0.1 fusion.29
  468.1 9.8 %fusion.33 = f32[512,8192]{1,0:T(8,128)} fusion(bf16[8192,128]{1,0:T(8,128)(2,1)} %all-gather.7.cloned.1.call-done, bf16[512,256]{1,0:T(8,128)(2,1)S(1)} %bitcast.180), kind=kOutput, calls=%fused_computation.52 | convolution fusion | flops 1073741824 | bytes 19005440 | tf_op jit(solution)/shard_map/dot_general | solution.py:131
  477.9 15.3 %add_convert_fusion = bf16[512,8192]{1,0:T(8,128)(2,1)} fusion(f32[512,8192]{1,0:T(8,128)} %fusion.21, f32[512,8192]{1,0:T(8,128)} %fusion.33, bf16[8192,128]{1,0:T(8,128)(2,1)S(1)} %copy-done.1, bf16[512,256]{1,0:T(8,128)(2,1)S(1)} %bitcast.181), kind=kOutput, calls=%fused_computation.3 | convolution fusion | flops 1086324736 | bytes 44171264 | tf_op jit(solution)/shard_map/dot_general | solution.py:134
  493.2 1.2 copy-done.3
  494.4 0.7 copy.24
  495.1 1.2 copy.77
  496.4 165.0 %reduce-scatter.2.cloned.1.call-done = bf16[512,1024]{1,0:T(8,128)(2,1)} async-done(((bf16[512,8192]{1,0:T(8,128)(2,1)}), bf16[512,1024]{1,0:T(8,128)(2,1)}) %reduce-scatter.2.cloned.1.call-update) | async-done | bytes 1048592 | tf_op jit(solution)/shard_map/reduce_scatter | solution.py:137
  (26 shorter events, 0.2 us)
Async XLA Ops:
  7.2 54.4 %all-gather.9.cloned.1.call-start = ((), (), s32[]{:S(2)}) async-start(), calls=%async_computation.3 | async-start | bytes 2228224 | tf_op jit(solution)/shard_map/all_gather | solution.py:42
  7.9 222.1 %all-gather.5.cloned.1.call-start = ((), (), s32[]{:S(2)}) async-start(), calls=%async_computation.1 | async-start | bytes 9437184 | tf_op jit(solution)/shard_map/all_gather | solution.py:39
  8.6 272.8 %all-gather.7.cloned.1.call-start = ((), (), s32[]{:S(2)}) async-start(), calls=%async_computation.2 | async-start | bytes 2228224 | tf_op jit(solution)/shard_map/all_gather | solution.py:41
  9.4 384.9 %all-gather.11.cloned.1.call-start = ((), (), s32[]{:S(2)}) async-start(), calls=%async_computation.4 | async-start | bytes 17825792 | tf_op jit(solution)/shard_map/all_gather | solution.py:40
  10.0 651.5 %reduce-scatter.2.cloned.1.call-start = ((), (), s32[]{:S(2)}) async-start(), calls=%async_computation.5 | async-start | bytes 9437184 | tf_op jit(solution)/shard_map/reduce_scatter | solution.py:137
  14.7 276.9 %copy-start.2 = (bf16[512,1024]{1,0:T(8,128)(2,1)S(1)}, bf16[512,1024]{1,0:T(8,128)(2,1)}, u32[]{:S(2)}) copy-start(bf16[512,1024]{1,0:T(8,128)(2,1)} %param.13) | copy-start | bytes 3145732
  288.3 10.5 %collective-permute-start.1 = (bf16[512,256]{0,1:T(8,128)(2,1)S(1)}, bf16[512,256]{0,1:T(8,128)(2,1)S(1)}, u32[]{:S(2)}, u32[]{:S(2)}) collective-permute-start(bf16[512,256]{0,1:T(8,128)(2,1)S(1)} %pad_maximum_fusion.2), channel_id=1, source_target_pairs={{8,0},{16,8},{24,16},{32,24},{40,32},{48,40},{56,48},{64,56},{72,6... | collective-permute-start | bytes 786440 | tf_op jit(solution)/shard_map/ppermute | solution.py:21
  288.6 12.9 %collective-permute-start = (bf16[512,256]{0,1:T(8,128)(2,1)S(1)}, bf16[512,256]{0,1:T(8,128)(2,1)S(1)}, u32[]{:S(2)}, u32[]{:S(2)}) collective-permute-start(bf16[512,256]{0,1:T(8,128)(2,1)S(1)} %pad_maximum_fusion.2), channel_id=1, source_target_pairs={{0,8},{8,16},{16,24},{24,32},{32,40},{40,48},{48,56},{56,64},{64,7... | collective-permute-start | bytes 786440 | tf_op jit(solution)/shard_map/ppermute | solution.py:18
  409.3 3.8 copy-start.4
  425.2 2.0 copy-start
  428.9 8.0 %copy-start.6 = (f32[4,512,1,128]{1,3,0,2:T(8,128)S(1)}, f32[4,512,1,128]{1,3,0,2:T(8,128)}, u32[]{:S(2)}) copy-start(f32[4,512,1,128]{1,3,0,2:T(8,128)} %fusion.18) | copy-start | bytes 3145732
  444.5 7.8 %copy-start.5 = (bf16[4,128,1,8,128]{4,3,1,0,2:T(8,128)(2,1)S(1)}, bf16[4,128,1,8,128]{4,3,1,0,2:T(8,128)(2,1)}, u32[]{:S(2)}) copy-start(bf16[4,128,1,8,128]{4,3,1,0,2:T(8,128)(2,1)} %copy.29) | copy-start | bytes 3145732
  449.0 19.0 %collective-permute-start.2 = (bf16[4,128,256]{2,1,0:T(8,128)(2,1)}, bf16[4,128,256]{2,1,0:T(8,128)(2,1)S(1)}, u32[]{:S(2)}, u32[]{:S(2)}) collective-permute-start(bf16[4,128,256]{2,1,0:T(8,128)(2,1)} %get-tuple-element.4), channel_id=1, source_target_pairs={{8,0},{16,8},{24,16},{32,24},{40,32},{48,40},{56,48},{64,56},{72,6... | collective-permute-start | bytes 786440 | tf_op jit(solution)/shard_map/ppermute | solution.py:29
  449.3 18.7 %collective-permute-start.3 = (bf16[4,128,256]{2,1,0:T(8,128)(2,1)S(1)}, bf16[4,128,256]{2,1,0:T(8,128)(2,1)S(1)}, u32[]{:S(2)}, u32[]{:S(2)}) collective-permute-start(bf16[4,128,256]{2,1,0:T(8,128)(2,1)S(1)} %get-tuple-element.5), channel_id=1, source_target_pairs={{120,0},{0,8},{8,16},{16,24},{24,32},{32,40},{40,48},{48,56},{56,6... | collective-permute-start | bytes 786440 | tf_op jit(solution)/shard_map/ppermute | solution.py:29
  468.1 9.8 %copy-start.1 = (bf16[8192,128]{1,0:T(8,128)(2,1)S(1)}, bf16[8192,128]{1,0:T(8,128)(2,1)}, u32[]{:S(2)}) copy-start(bf16[8192,128]{1,0:T(8,128)(2,1)} %all-gather.9.cloned.1.call-done) | copy-start | bytes 6291460
  493.2 1.2 copy-start.3
Sparse Core Ops, SparseCore 0:
  10.5 51.0 all-gather.8
  63.2 166.7 all-gather.4
  232.4 48.9 all-gather.6
  283.7 110.4 all-gather.10
  493.4 168.0 reduce-scatter.1
where the time goes:
time: 668 us
  waiting for transfers between devices  526 us (79%)
  matrix products  88 us (13%)
  local copies, waits for them, and re-layouts  22.9 us (3%)
  between operations  14 us (2%)
  other arithmetic  9.83 us (1%)
  starting transfers between devices  6.76 us (1%)
    all_gather x1, waiting for transfers between devices, body(): all_features = lax.all_gather(layer_input, 'col', axis=1, tiled=True)  168 us
    reduce_scatter x1, waiting for transfers between devices, body(): lax.psum_scatter(partial_grad.astype(jnp.bfloat16), 'col', scatter_dimens...  165 us
    all_gather x1, waiting for transfers between devices, body(): full_query = lax.all_gather(w_query, 'row', axis=0, tiled=True)  91 us
    all_gather x1, waiting for transfers between devices, body(): full_value = lax.all_gather(w_value, 'row', axis=0, tiled=True)  46.9 us
    all_gather x1, waiting for transfers between devices, body(): full_key = lax.all_gather(w_key, 'row', axis=0, tiled=True)  44.6 us
    dot_general x1, matrix products, body(): lax.dot_general(grad_query, full_query, contract, preferred_element_type=...  15.7 us
    dot_general x1, matrix products, body(): lax.dot_general(grad_values, full_value, contract, preferred_element_type...  15.3 us
    dot_general x1, matrix products, body(): jnp.dot(all_features, full_query, preferred_element_type=jnp.float32)  14.8 us
  transfers between devices with their start and end apart: 9, of which 7 were waited for; matrix products, arithmetic and copies ran while one was open for 6% of the time, Pallas kernels for 0%

commit v1 on v0

--- a/solution.py
+++ b/solution.py
@@ -39,7 +39,10 @@
     all_features = lax.all_gather(layer_input, "col", axis=1, tiled=True)
     full_query = lax.all_gather(w_query, "row", axis=0, tiled=True)
     full_key = lax.all_gather(w_key, "row", axis=0, tiled=True)
-    full_value = lax.all_gather(w_value, "row", axis=0, tiled=True)
+    size = lax.axis_size("row")
+    tiles = jnp.stack([w_value for _ in range(size)])
+    tiles = lax.all_to_all(tiles, "row", split_axis=0, concat_axis=0)
+    full_value = jnp.concatenate(tiles, axis=0)
     query = jnp.dot(all_features, full_query, preferred_element_type=jnp.float32).astype(
         jnp.bfloat16
     )

time: 668 us -> 634 us (0.949)
  waiting for transfers between devices: 526 us -> 479 us
  starting transfers between devices: 6.76 us -> 15.1 us
    all_gather x1 -> x0, waiting for transfers between devices: 46.9 us -> none  [body(): full_value = lax.all_gather(w_value, 'row', axis=0, tiled=True)]
    all_to_all x0 -> x1, starting transfers between devices: none -> 8.45 us  [body(): tiles = lax.all_to_all(tiles, 'row', split_axis=0, concat_axis=0)]
    all_gather x1, waiting for transfers between devices: 91 us -> 84.2 us  [body(): full_query = lax.all_gather(w_query, 'row', axis=0, tiled=True)]
  transfers between devices with their start and end apart: 9 -> 9, of which waited for: 7 -> 5; matrix products, arithmetic and copies ran while one was open for 6% -> 7% of each run, Pallas kernels for 0% -> 0%
where the time goes in v1:
time: 634 us
  waiting for transfers between devices  479 us (76%)
  matrix products  88.1 us (14%)
  local copies, waits for them, and re-layouts  26.7 us (4%)
  starting transfers between devices  15.1 us (2%)
  between operations  14 us (2%)
  other arithmetic  10.4 us (2%)
    all_gather x1, waiting for transfers between devices, body(): all_features = lax.all_gather(layer_input, 'col', axis=1, tiled=True)  168 us
    reduce_scatter x1, waiting for transfers between devices, body(): lax.psum_scatter(partial_grad.astype(jnp.bfloat16), 'col', scatter_dimens...  165 us
    all_gather x1, waiting for transfers between devices, body(): full_query = lax.all_gather(w_query, 'row', axis=0, tiled=True)  84.2 us
    all_gather x1, waiting for transfers between devices, body(): full_key = lax.all_gather(w_key, 'row', axis=0, tiled=True)  51.1 us
    dot_general x1, matrix products, body(): lax.dot_general(grad_query, full_query, contract, preferred_element_type=...  15.7 us
    dot_general x1, matrix products, body(): lax.dot_general(grad_values, full_value, contract, preferred_element_type...  15.3 us
    dot_general x1, matrix products, body(): jnp.dot(all_features, full_query, preferred_element_type=jnp.float32)  14.8 us
  transfers between devices with their start and end apart: 9, of which 5 were waited for; matrix products, arithmetic and copies ran while one was open for 7% of the time, Pallas kernels for 0%

profile of v1, /device:TPU:1, one launch (start us, length us, event | category | flops | bytes accessed | tf_op | source)
XLA Modules:
  0.0 633.8 jit_solution(8201716171322576729)
XLA Ops:
  7.2 0.0 all-gather.6.cloned.1.call-start
  7.2 0.7 all-gather.6.cloned.1.call-update
  7.9 0.0 all-gather.4.cloned.1.call-start
  8.0 0.7 all-gather.4.cloned.1.call-update
  8.7 0.0 all-gather.8.cloned.1.call-start
  8.7 0.7 all-gather.8.cloned.1.call-update
  9.4 2.7 stack.2
  12.1 8.4 %all-to-all-start = ((bf16[16,512,128]{2,1,0:T(8,128)(2,1)}), bf16[16,512,128]{2,1,0:T(8,128)(2,1)S(1)}, u32[]{:S(2)}, u32[]{:S(2)}) async-start(bf16[16,512,128]{2,1,0:T(8,128)(2,1)} %stack.2), calls=%async_computation | async-start | bytes 4194304 | tf_op jit(solution)/shard_map/all_to_all | solution.py:44
  20.5 0.0 reduce-scatter.2.cloned.1.call-start
  20.6 0.1 reshape.236
  20.7 0.1 reshape.221
  20.8 0.1 reshape.228
  20.9 0.1 dynamic_slice.3
  21.0 0.7 gather_fusion.1
  21.6 0.1 reshape.235
  21.7 0.1 broadcast_bitcast_fusion.1
  21.8 0.1 fusion.36
  21.9 0.1 broadcast_bitcast_fusion
  22.0 51.1 %all-gather.6.cloned.1.call-done = bf16[8192,128]{1,0:T(8,128)(2,1)} async-done(((bf16[512,128]{1,0:T(8,128)(2,1)}), bf16[8192,128]{1,0:T(8,128)(2,1)}) %all-gather.6.cloned.1.call-update) | async-done | bytes 2097168 | tf_op jit(solution)/shard_map/all_gather | solution.py:41
  73.0 168.4 %all-gather.4.cloned.1.call-done = bf16[512,8192]{1,0:T(8,128)(2,1)} async-done(((bf16[512,1024]{1,0:T(8,128)(2,1)}), bf16[512,8192]{1,0:T(8,128)(2,1)}) %all-gather.4.cloned.1.call-update) | async-done | bytes 8388624 | tf_op jit(solution)/shard_map/all_gather | solution.py:39
  241.5 6.8 %convolution_convert_fusion.3 = bf16[512,128]{0,1:T(8,128)(2,1)S(1)} fusion(bf16[512,8192]{1,0:T(8,128)(2,1)} %all-gather.4.cloned.1.call-done, bf16[8192,128]{1,0:T(8,128)(2,1)} %all-gather.6.cloned.1.call-done), kind=kOutput, calls=%fused_computation.32 | convolution fusion | flops 1073807360 | bytes 10616832 | tf_op jit(solution)/shard_map/dot_general | solution.py:49
  248.3 7.1 %convolution_convert_fusion.2 = bf16[512,128]{0,1:T(8,128)(2,1)S(1)} fusion(bf16[512,8192]{1,0:T(8,128)(2,1)} %all-gather.4.cloned.1.call-done, bf16[8192,128]{1,0:T(8,128)(2,1)S(1)} %bitcast.174), kind=kOutput, calls=%fused_computation.31 | convolution fusion | flops 1073807360 | bytes 10616832 | tf_op jit(solution)/shard_map/dot_general | solution.py:50
  255.4 0.7 pad_maximum_fusion.2
  256.1 0.7 collective-permute-start.1
  256.8 2.6 collective-permute-start
  259.4 1.5 copy.63
  260.9 1.6 copy.25
  262.5 8.6 %collective-permute-done.1 = bf16[512,256]{0,1:T(8,128)(2,1)} collective-permute-done((bf16[512,256]{0,1:T(8,128)(2,1)}, bf16[512,256]{0,1:T(8,128)(2,1)}, u32[]{:S(2)}, u32[]{:S(2)}) %collective-permute-start.1) | collective-permute-done | bytes 262176 | tf_op jit(solution)/shard_map/ppermute | solution.py:21
  271.2 2.0 pad_maximum_fusion.1
  273.1 1.4 copy.19
  274.6 0.6 gather_fusion
  275.2 0.3 gather.11
  275.5 0.5 copy_select_fusion
  276.0 84.2 %all-gather.8.cloned.1.call-done = bf16[8192,1024]{1,0:T(8,128)(2,1)} async-done(((bf16[512,1024]{1,0:T(8,128)(2,1)}), bf16[8192,1024]{1,0:T(8,128)(2,1)}) %all-gather.8.cloned.1.call-update) | async-done | bytes 16777232 | tf_op jit(solution)/shard_map/all_gather | solution.py:40
  360.2 14.8 %fusion.16 = bf16[64,8,8,128]{3,1,2,0:T(8,128)(2,1)S(1)} fusion(bf16[512,8192]{1,0:T(8,128)(2,1)} %all-gather.4.cloned.1.call-done, bf16[8192,1024]{1,0:T(8,128)(2,1)} %all-gather.8.cloned.1.call-done), kind=kOutput, calls=%fused_computation.27 | convolution fusion | flops 8590458880 | bytes 26214400 | tf_op jit(solution)/shard_map/dot_general | solution.py:46
  375.0 0.3 copy.61
  375.2 1.9 bitcast_reduce_fusion
  377.1 1.9 fusion.5
  379.1 4.3 fusion.18
  383.4 4.0 fusion.12
  387.3 3.7 fusion.6
  391.1 2.0 copy-done.1
  393.0 1.8 fusion.17
  394.8 8.0 %copy.49 = bf16[4,8,128,512]{3,1,2,0:T(8,128)(2,1)} copy(bf16[4,8,128,512]{2,3,1,0:T(8,128)(2,1)} %copy-done.1) | data formatting | bytes 8388608 | tf_op jit(solution)/shard_map/reshape.36
  402.8 0.3 copy.34
  403.1 3.1 convolution_bitcast_fusion
  406.2 0.3 copy.32
  406.5 2.4 copy.29
  408.9 1.5 pad_maximum_fusion
  410.4 0.1 broadcast_in_dim.52
  410.6 3.5 scatter_fusion
  414.1 0.1 convert.8
  414.2 0.7 fusion.42
  414.9 0.2 collective-permute-start.2
  415.2 3.0 collective-permute-start.3
  418.2 15.7 %fusion.21 = f32[512,8192]{1,0:T(8,128)} fusion(bf16[8192,1024]{1,0:T(8,128)(2,1)} %all-gather.8.cloned.1.call-done, bf16[64,8,8,128]{3,2,1,0:T(8,128)(2,1)S(1)} %bitcast.187), kind=kOutput, calls=%fused_computation.33 | convolution fusion | flops 8589934592 | bytes 34603008 | tf_op jit(solution)/shard_map/dot_general | solution.py:131
  433.8 0.1 fusion.29
  433.9 9.8 %fusion.33 = f32[512,8192]{1,0:T(8,128)} fusion(bf16[8192,128]{1,0:T(8,128)(2,1)} %all-gather.6.cloned.1.call-done, bf16[512,256]{1,0:T(8,128)(2,1)S(1)} %bitcast.183), kind=kOutput, calls=%fused_computation.52 | convolution fusion | flops 1073741824 | bytes 19005440 | tf_op jit(solution)/shard_map/dot_general | solution.py:134
  443.8 15.3 %add_convert_fusion = bf16[512,8192]{1,0:T(8,128)(2,1)} fusion(f32[512,8192]{1,0:T(8,128)} %fusion.21, f32[512,8192]{1,0:T(8,128)} %fusion.33, bf16[8192,128]{1,0:T(8,128)(2,1)S(1)} %bitcast.175, bf16[512,256]{1,0:T(8,128)(2,1)S(1)} %bitcast.184), kind=kOutput, calls=%fused_computation.3 | convolution fusion | flops 1086324736 | bytes 44171264 | tf_op jit(solution)/shard_map/dot_general | solution.py:137
  459.1 0.0 reduce-scatter.2.cloned.1.call-update
  459.1 1.2 copy-done.4
  460.3 0.7 copy.24
  461.0 1.2 copy.77
  462.2 165.0 %reduce-scatter.2.cloned.1.call-done = bf16[512,1024]{1,0:T(8,128)(2,1)} async-done(((bf16[512,8192]{1,0:T(8,128)(2,1)}), bf16[512,1024]{1,0:T(8,128)(2,1)}) %reduce-scatter.2.cloned.1.call-update) | async-done | bytes 1048592 | tf_op jit(solution)/shard_map/reduce_scatter | solution.py:140
  (30 shorter events, 0.1 us)
Async XLA Ops:
  7.2 13.4 %copy-start.8 = (s32[4,4]{1,0:T(4,128)S(1)}, s32[4,4]{1,0:T(4,128)}, u32[]{:S(2)}) copy-start(s32[4,4]{1,0:T(4,128)} %param.12) | copy-start | bytes 196
  7.2 13.7 %copy-start = (s32[64]{0:T(128)S(1)}, s32[64]{0:T(128)}, u32[]{:S(2)}) copy-start(s32[64]{0:T(128)} %param.11) | copy-start | bytes 772
  7.2 65.9 %all-gather.6.cloned.1.call-start = ((), (), s32[]{:S(2)}) async-start(), calls=%async_computation.3 | async-start | bytes 2228224 | tf_op jit(solution)/shard_map/all_gather | solution.py:41
  7.9 233.5 %all-gather.4.cloned.1.call-start = ((), (), s32[]{:S(2)}) async-start(), calls=%async_computation.2 | async-start | bytes 9437184 | tf_op jit(solution)/shard_map/all_gather | solution.py:39
  8.7 351.5 %all-gather.8.cloned.1.call-start = ((), (), s32[]{:S(2)}) async-start(), calls=%async_computation.4 | async-start | bytes 17825792 | tf_op jit(solution)/shard_map/all_gather | solution.py:40
  12.1 236.2 %all-to-all-start = ((bf16[16,512,128]{2,1,0:T(8,128)(2,1)}), bf16[16,512,128]{2,1,0:T(8,128)(2,1)S(1)}, u32[]{:S(2)}, u32[]{:S(2)}) async-start(bf16[16,512,128]{2,1,0:T(8,128)(2,1)} %stack.2), calls=%async_computation | async-start | bytes 4194304 | tf_op jit(solution)/shard_map/all_to_all | solution.py:44
  20.5 606.7 %reduce-scatter.2.cloned.1.call-start = ((), (), s32[]{:S(2)}) async-start(), calls=%async_computation.5 | async-start | bytes 9437184 | tf_op jit(solution)/shard_map/reduce_scatter | solution.py:140
  248.3 24.8 %copy-start.2 = (bf16[16,512,128]{2,1,0:T(8,128)(2,1)}, bf16[16,512,128]{2,1,0:T(8,128)(2,1)S(1)}, u32[]{:S(2)}) copy-start(bf16[16,512,128]{2,1,0:T(8,128)(2,1)S(1)} %all-to-all-done) | copy-start | bytes 6291460
  256.1 15.0 %collective-permute-start.1 = (bf16[512,256]{0,1:T(8,128)(2,1)}, bf16[512,256]{0,1:T(8,128)(2,1)}, u32[]{:S(2)}, u32[]{:S(2)}) collective-permute-start(bf16[512,256]{0,1:T(8,128)(2,1)} %pad_maximum_fusion.2), channel_id=1, source_target_pairs={{8,0},{16,8},{24,16},{32,24},{40,32},{48,40},{56,48},{64,56},{72,6... | collective-permute-start | bytes 786440 | tf_op jit(solution)/shard_map/ppermute | solution.py:21
  256.8 14.4 %collective-permute-start = (bf16[512,256]{0,1:T(8,128)(2,1)}, bf16[512,256]{0,1:T(8,128)(2,1)}, u32[]{:S(2)}, u32[]{:S(2)}) collective-permute-start(bf16[512,256]{0,1:T(8,128)(2,1)} %pad_maximum_fusion.2), channel_id=1, source_target_pairs={{0,8},{8,16},{16,24},{24,32},{32,40},{40,48},{48,56},{56,64},{64,7... | collective-permute-start | bytes 786440 | tf_op jit(solution)/shard_map/ppermute | solution.py:18
  375.2 3.8 copy-start.5
  391.0 2.0 copy-start.1
  394.8 8.0 %copy-start.7 = (f32[4,512,1,128]{1,3,0,2:T(8,128)S(1)}, f32[4,512,1,128]{1,3,0,2:T(8,128)}, u32[]{:S(2)}) copy-start(f32[4,512,1,128]{1,3,0,2:T(8,128)} %fusion.18) | copy-start | bytes 3145732
  410.4 7.8 %copy-start.6 = (bf16[4,128,1,8,128]{4,3,1,0,2:T(8,128)(2,1)S(1)}, bf16[4,128,1,8,128]{4,3,1,0,2:T(8,128)(2,1)}, u32[]{:S(2)}) copy-start(bf16[4,128,1,8,128]{4,3,1,0,2:T(8,128)(2,1)} %copy.29) | copy-start | bytes 3145732
  414.9 18.9 %collective-permute-start.2 = (bf16[4,128,256]{2,1,0:T(8,128)(2,1)}, bf16[4,128,256]{2,1,0:T(8,128)(2,1)S(1)}, u32[]{:S(2)}, u32[]{:S(2)}) collective-permute-start(bf16[4,128,256]{2,1,0:T(8,128)(2,1)} %get-tuple-element.4), channel_id=1, source_target_pairs={{8,0},{16,8},{24,16},{32,24},{40,32},{48,40},{56,48},{64,56},{72,6... | collective-permute-start | bytes 786440 | tf_op jit(solution)/shard_map/ppermute | solution.py:29
  415.2 18.7 %collective-permute-start.3 = (bf16[4,128,256]{2,1,0:T(8,128)(2,1)S(1)}, bf16[4,128,256]{2,1,0:T(8,128)(2,1)S(1)}, u32[]{:S(2)}, u32[]{:S(2)}) collective-permute-start(bf16[4,128,256]{2,1,0:T(8,128)(2,1)S(1)} %get-tuple-element.5), channel_id=1, source_target_pairs={{120,0},{0,8},{8,16},{16,24},{24,32},{32,40},{40,48},{48,56},{56,6... | collective-permute-start | bytes 786440 | tf_op jit(solution)/shard_map/ppermute | solution.py:29
  433.9 9.8 %copy-start.3 = (bf16[16,512,128]{2,1,0:T(8,128)(2,1)S(1)}, bf16[16,512,128]{2,1,0:T(8,128)(2,1)}, u32[]{:S(2)}) copy-start(bf16[16,512,128]{2,1,0:T(8,128)(2,1)} %copy-done.2) | copy-start | bytes 6291460
  459.1 1.2 copy-start.4
Sparse Core Ops, SparseCore 0:
  10.5 62.5 all-gather.5
  74.7 166.7 all-gather.3
  243.9 116.2 all-gather.7
  459.2 168.0 reduce-scatter.1
